TPU v7x, 32 devices: a whole 2x2x4 slice. The times are simulated.
32 devices in a mesh: dp: 2 (over core), seq: 4 (over y, x), head: 4 (over z).
Axes of the slice: x: 2, y: 2, z: 4, core: 2. Of those that a mesh axis runs over, the one named last changes fastest.
Arguments:
- query_rows: bfloat16 [2, 2048, 4096], P('dp', 'seq', 'head'), may hold values from -1.796875 to 1.796875
- key_rows: bfloat16 [2, 2048, 4096], P('dp', 'seq', 'head'), may hold values from -1.796875 to 1.796875
- value_rows: bfloat16 [2, 2048, 4096], P('dp', 'seq', 'head'), may hold values from -6 to 6
- norm_gain: float32 [4096], P('head'), may hold values from 0.1 to 1.9
- cotangent: bfloat16 [2, 2048, 4096], P('dp', 'seq', 'head'), may hold values from -10 to 10
- loss_mask: int32 [2, 2048], P('dp', 'seq'), may hold values 0 or 1
- importance: float32 [2, 2048], P('dp', 'seq'), may hold values from 0.5 to 2
- advantage: float32 [2], P('dp'), may hold values from -3 to 3
- lengths: int32 [2], P('dp'), may hold values from 512 to 2048, as said below
- decay_index: int32 [32], P('head'), may hold values from 0 to 11
Outputs:
- mixed: bfloat16 [2, 2048, 4096], P('dp', 'seq', 'head')
- query_grad: bfloat16 [2, 2048, 4096], P('dp', 'seq', 'head')
- key_grad: bfloat16 [2, 2048, 4096], P('dp', 'seq', 'head')
- value_grad: bfloat16 [2, 2048, 4096], P('dp', 'seq', 'head')
- gain_grad: float32 [4096], P('head')
Inputs may be any that keep to these rules, and one draw needn't show every extreme that they name: `lengths`: at least one response has length 2048.
All inputs are finite; a program needn't handle non-finite values. No bound on the sum of `loss_mask` on one device may be relied on, other than what follows from the above.
Results may differ from a plain program's by a relative error of at most 0.0063.
Values sent between devices are 32-bit elements; how exact they have to be, the bound alone decides.
A program may use at most 128 MiB of HBM per device.

v0:
```python
import functools

import jax
import jax.numpy as jnp
from jax import lax
from jax.experimental import pallas as pl
from jax.experimental.pallas import tpu as pltpu
from jax.sharding import PartitionSpec as P

clip_high = 1.28
epsilon = 1e-06
f32 = jnp.float32
bf16 = jnp.bfloat16
MESH = pl.DeviceIdType.MESH


def dot(a, b, ca, cb):
    return lax.dot_general(a, b, (((ca,), (cb,)), ((), ())), preferred_element_type=f32)


def kernel(
    n_seq,
    n_head,
    n_dp,
    decay_hbm,
    adv_ref,
    len_ref,
    gain_hbm,
    mask_hbm,
    imp_hbm,
    q_hbm,
    k_hbm,
    v_hbm,
    c_hbm,
    o_mix,
    o_dq,
    o_dk,
    o_dv,
    gg_ref,
    decay_ref,
    gain_ref,
    mask_ref,
    imp_ref,
    q,
    k,
    v,
    c,
    out,
    go,
    pk,
    pv,
    probs,
    dsc,
    wtab,
    up,
    down,
    squares,
    mixes,
    tot_f,
    rcv_f,
    tot_b,
    rcv_b,
    pref,
    state,
    stat,
    gsum,
    grcv,
    in_sem,
    small_sem,
    fs_sem,
    fr_sem,
    bs_sem,
    br_sem,
    ss_sem,
    sr_sem,
    gs_sem,
    gr_sem,
):
    slab, features = q.shape
    heads = decay_ref.shape[0]
    dim = features // heads
    blk = min(256, slab)
    nblk = slab // blk
    stages = n_seq.bit_length() - 1
    me = lax.axis_index("seq")
    mh = lax.axis_index("head")
    md = lax.axis_index("dp")

    def partner(step):
        g = 1 << step
        bit = lax.rem(lax.div(me, g), 2)
        return me + g * (1 - 2 * bit)

    loads = [
        pltpu.make_async_copy(src.at[0], dst, in_sem.at[i])
        for i, (src, dst) in enumerate(((k_hbm, k), (v_hbm, v), (q_hbm, q), (c_hbm, c)))
    ]
    small = [
        pltpu.make_async_copy(src, dst, small_sem.at[i])
        for i, (src, dst) in enumerate(
            (
                (decay_hbm, decay_ref),
                (gain_hbm, gain_ref),
                (mask_hbm, mask_ref),
                (imp_hbm, imp_ref),
            )
        )
    ]
    for load in small + loads:
        load.start()

    barrier = pltpu.get_barrier_semaphore()
    for s in range(stages):
        pl.semaphore_signal(barrier, inc=1, device_id={"seq": partner(s)}, device_id_type=MESH)
    for off in range(1, n_head):
        pl.semaphore_signal(
            barrier, inc=1, device_id={"head": lax.rem(mh + off, n_head)}, device_id_type=MESH
        )
    for off in range(1, n_dp):
        pl.semaphore_signal(
            barrier, inc=1, device_id={"dp": lax.rem(md + off, n_dp)}, device_id_type=MESH
        )

    def cols(h):
        return pl.ds(pl.multiple_of(h * dim, dim), dim)

    def rate(h, width):
        index = jnp.full((1, width), decay_ref[h], jnp.int32).astype(f32)
        return 16.0 / (slab * jnp.exp2(index))

    small[0].wait()
    base = min(128, slab)
    line = lax.broadcasted_iota(jnp.int32, (base, dim), 0).astype(f32)

    @pl.loop(0, heads)
    def _(h):
        r = rate(h, dim)
        rise = jnp.exp2(-r * line)
        fall = jnp.exp2(-r * (base - 1.0 - line))
        for b in range(slab // base):
            rows = pl.ds(b * base, base)
            up[h, rows, :] = rise * jnp.exp2(-r * float(b * base))
            down[h, rows, :] = fall * jnp.exp2(-r * float(slab - (b + 1) * base))

    pl.semaphore_wait(barrier, stages + n_head - 1 + n_dp - 1)

    def fwd_copy(s, h):
        return pltpu.make_async_remote_copy(
            src_ref=tot_f.at[s, h],
            dst_ref=rcv_f.at[s, h],
            send_sem=fs_sem.at[s, h],
            recv_sem=fr_sem.at[s, h],
            device_id={"seq": partner(s)},
            device_id_type=MESH,
        )

    def bwd_copy(s, h):
        return pltpu.make_async_remote_copy(
            src_ref=tot_b.at[s, h],
            dst_ref=rcv_b.at[s, h],
            send_sem=bs_sem.at[s, h],
            recv_sem=br_sem.at[s, h],
            device_id={"seq": partner(s)},
            device_id_type=MESH,
        )

    def lower_only(s, place):
        return lax.div(place, 2 << s) == n_seq // (2 << s) - 1

    def is_upper(s, place):
        return lax.rem(lax.div(place, 1 << s), 2) == 1

    def sends(s, place):
        return jnp.logical_not(jnp.logical_and(is_upper(s, place), lower_only(s, place)))

    def takes(s, place):
        return jnp.logical_or(is_upper(s, place), jnp.logical_not(lower_only(s, place)))

    def begin(copy, s, h, place):
        @pl.when(sends(s, place))
        def _():
            copy(s, h).start()

    def settle(copy, place):
        for s in range(stages):

            @pl.when(sends(s, place))
            def _(s=s):
                @pl.loop(0, heads)
                def _(h):
                    copy(s, h).wait_send()

    def accept(copy, h, s, place, tot, rcv):
        first = s == 0
        if first:

            @pl.when(jnp.logical_not(takes(s, place)))
            def _():
                pref[h] = jnp.zeros((dim, dim), f32)

        @pl.when(takes(s, place))
        def _():
            copy(s, h).wait_recv()
            merge(h, s, place, tot, rcv, first)

        if s + 1 < stages:
            begin(copy, s + 1, h, place)

    def merge(h, s, place, tot, rcv, first):
        g = 1 << s
        r = rate(h, dim) * slab
        upper = jnp.full((1, dim), lax.rem(lax.div(place, g), 2), jnp.int32).astype(f32)
        inner = jnp.full((1, dim), lax.rem(place, g), jnp.int32).astype(f32)
        got = rcv[s, h]
        to_prefix = upper * jnp.exp2(-r * inner)
        if first:
            pref[h] = to_prefix * got
        else:
            pref[h] = pref[h] + to_prefix * got
        if s + 1 < stages:
            whole = jnp.exp2(-r * g)
            from_got = upper * whole + (1.0 - upper)
            from_own = upper + (1.0 - upper) * whole
            tot[s + 1, h] = from_got * got + from_own * tot[s, h]

    loads[0].wait()
    loads[1].wait()

    @pl.loop(0, heads)
    def _(h):
        faded = (k[:, cols(h)].astype(f32) * down[h]).astype(bf16)
        tot_f[0, h] = dot(faded, v[:, cols(h)], 0, 0)
        begin(fwd_copy, 0, h, me)

    loads[2].wait()

    t_at = lax.broadcasted_iota(jnp.int32, (blk, blk), 0)
    s_at = lax.broadcasted_iota(jnp.int32, (blk, blk), 1)

    @pl.loop(0, heads)
    def _(h):
        r = rate(h, dim)
        place = lax.broadcasted_iota(jnp.int32, (1, dim), 1).astype(f32)
        front = up[h, pl.ds(0, blk), :]
        near = jnp.concatenate(
            [front * jnp.exp2(r * (place + float(b * dim))) for b in range(blk // dim)], axis=1
        )
        wtab[h, 0] = jnp.where(t_at >= s_at, near, 0.0)
        for d in range(1, nblk):
            far = jnp.exp2(-r * float(blk * d))
            wtab[h, d] = near * jnp.concatenate([far] * (blk // dim), axis=1)
        for i in range(nblk):
            rows = pl.ds(i * blk, blk)
            for j in range(i + 1):
                past = pl.ds(j * blk, blk)
                score = dot(q[rows, cols(h)], k[past, cols(h)], 1, 1)
                probs[h, rows, past] = (score * wtab[h, i - j]).astype(bf16)
            past = pl.ds(0, (i + 1) * blk)
            out[rows, cols(h)] = dot(probs[h, rows, past], v[past, cols(h)], 1, 0)
        accept(fwd_copy, h, 0, me, tot_f, rcv_f)

    for s in range(1, stages - 1):

        @pl.loop(0, heads)
        def _(h, s=s):
            accept(fwd_copy, h, s, me, tot_f, rcv_f)

    loads[3].wait()
    for load in small[1:]:
        load.wait()

    token = mask_ref[...].astype(f32)
    at = me * slab + lax.broadcasted_iota(jnp.int32, (1, slab), 1)
    length = jnp.full((1, slab), len_ref[0], jnp.int32)
    token = token * (at < length).astype(f32) * jnp.minimum(imp_ref[...], clip_high)
    token = token * adv_ref[0] * (float(slab * n_seq) / length.astype(f32))

    squares[...] = jnp.zeros((slab, dim), f32)
    mixes[...] = jnp.zeros((slab, dim), f32)

    @pl.loop(0, heads)
    def _(h):
        if stages > 1:
            accept(fwd_copy, h, stages - 1, me, tot_f, rcv_f)
        half = pref[h].astype(bf16)
        state[h] = half
        grow = up[h] * jnp.exp2(-rate(h, dim))
        full = out[:, cols(h)] + dot(q[:, cols(h)], half, 1, 0) * grow
        out[:, cols(h)] = full
        gain = gain_ref[pl.ds(h, 1), :]
        squares[...] += full * full
        mixes[...] += c[:, cols(h)].astype(f32) * gain * full

    stat[mh, 0:1, :] = jnp.sum(squares[...].T, axis=0, keepdims=True)
    stat[mh, 1:2, :] = jnp.sum(mixes[...].T, axis=0, keepdims=True) * token
    posts = [
        pltpu.make_async_remote_copy(
            src_ref=stat.at[mh],
            dst_ref=stat.at[mh],
            send_sem=ss_sem.at[off - 1],
            recv_sem=sr_sem.at[off - 1],
            device_id={"head": lax.rem(mh + off, n_head)},
            device_id_type=MESH,
        )
        for off in range(1, n_head)
    ]
    for post in posts:
        post.start()
    settle(fwd_copy, me)
    for post in posts:
        post.wait()
    sums = stat[0]
    for i in range(1, n_head):
        sums = sums + stat[i]
    count = features * n_head
    inverse = lax.rsqrt(sums[0:1] / count + epsilon)
    mean = inverse * (sums[1:2] / count)

    def column(row):
        return jnp.broadcast_to(row, (dim, slab)).T

    back = n_seq - 1 - me
    inv_col = column(inverse)
    give_col = column(inverse * token)
    take_col = column(inverse * inverse * mean)

    @pl.loop(0, heads)
    def _(h):
        gain = gain_ref[pl.ds(h, 1), :]
        full = out[:, cols(h)]
        given = c[:, cols(h)].astype(f32) * give_col
        o_mix[0, :, cols(h)] = (full * inv_col * gain).astype(bf16)
        gsum[0, pl.ds(h, 1), :] = jnp.sum(given * full, axis=0, keepdims=True)
        grad = (given * gain - take_col * full).astype(bf16)
        go[:, cols(h)] = grad
        faded = (q[:, cols(h)].astype(f32) * up[h]).astype(bf16)
        tot_b[0, h] = dot(faded, grad, 0, 0)
        begin(bwd_copy, 0, h, back)

    def gain_copy(s):
        target = {"dp": lax.rem(md + 1, n_dp)} if s == stages else {"seq": partner(s)}
        return pltpu.make_async_remote_copy(
            src_ref=gsum.at[s],
            dst_ref=grcv.at[s],
            send_sem=gs_sem.at[s],
            recv_sem=gr_sem.at[s],
            device_id=target,
            device_id_type=MESH,
        )

    gain_copy(0).start()

    @pl.loop(0, heads)
    def _(h):
        for i in range(nblk):
            rows = pl.ds(i * blk, blk)
            grad = go[rows, cols(h)]
            for j in range(i + 1):
                past = pl.ds(j * blk, blk)
                score = dot(grad, v[past, cols(h)], 1, 1)
                dsc[rows, past] = (score * wtab[h, i - j]).astype(bf16)
            past = pl.ds(0, (i + 1) * blk)
            grow = up[h, rows, :] * jnp.exp2(-rate(h, dim))
            total = dot(dsc[rows, past], k[past, cols(h)], 1, 0)
            total = total + dot(grad, state[h], 1, 1) * grow
            o_dq[0, rows, cols(h)] = total.astype(bf16)
        for j in range(nblk):
            past = pl.ds(j * blk, blk)
            rest = pl.ds(j * blk, slab - j * blk)
            pk[past, cols(h)] = dot(dsc[rest, past], q[rest, cols(h)], 0, 0)
            pv[past, cols(h)] = dot(probs[h, rest, past], go[rest, cols(h)], 0, 0)
        accept(bwd_copy, h, 0, back, tot_b, rcv_b)

    rounds = stages + (1 if n_dp > 1 else 0)
    for s in range(rounds):
        gain_copy(s).wait()
        gsum[s + 1] = gsum[s] + grcv[s]
        if s + 1 < rounds:
            gain_copy(s + 1).start()
    gg_ref[...] = gsum[rounds]

    for s in range(1, stages - 1):

        @pl.loop(0, heads)
        def _(h, s=s):
            accept(bwd_copy, h, s, back, tot_b, rcv_b)

    @pl.loop(0, heads)
    def _(h):
        if stages > 1:
            accept(bwd_copy, h, stages - 1, back, tot_b, rcv_b)
        half = pref[h].astype(bf16)
        fade = down[h] * jnp.exp2(-rate(h, dim))
        dk = pk[:, cols(h)] + dot(v[:, cols(h)], half, 1, 1) * fade
        o_dk[0, :, cols(h)] = dk.astype(bf16)
        dv = pv[:, cols(h)] + dot(k[:, cols(h)], half, 1, 0) * fade
        o_dv[0, :, cols(h)] = dv.astype(bf16)

    settle(bwd_copy, back)


def writer(n, *refs):
    sem = refs[-1]
    copies = [pltpu.make_async_copy(refs[i], refs[n + i], sem.at[i]) for i in range(n)]
    for copy in copies:
        copy.start()
    for copy in copies:
        copy.wait()


def on_device(
    n_seq,
    n_head,
    n_dp,
    query_rows,
    key_rows,
    value_rows,
    norm_gain,
    cotangent,
    loss_mask,
    importance,
    advantage,
    lengths,
    decay_index,
):
    batches, slab, features = query_rows.shape
    heads = decay_index.shape[0]
    dim = features // heads
    stages = n_seq.bit_length() - 1
    assert batches == 1 and n_seq == 1 << stages and stages > 0 and n_dp <= 2
    vmem = pl.BlockSpec(memory_space=pltpu.VMEM)
    smem = pl.BlockSpec(memory_space=pltpu.SMEM)
    far = pl.BlockSpec(memory_space=pltpu.HBM)
    rows = jax.ShapeDtypeStruct(query_rows.shape, bf16)
    wide = pltpu.VMEM((slab, features), bf16)
    wide32 = pltpu.VMEM((slab, features), f32)
    blk = min(256, slab)
    states = pltpu.VMEM((stages, heads, dim, dim), f32)
    dma = pltpu.SemaphoreType.DMA

    def stay(array):
        return pltpu.with_memory_space_constraint(array, pltpu.HBM)

    results = pl.pallas_call(
        functools.partial(kernel, n_seq, n_head, n_dp),
        out_shape=(rows, rows, rows, rows, jax.ShapeDtypeStruct((heads, dim), f32)),
        in_specs=[far, smem, smem] + [far] * 7,
        out_specs=(vmem,) * 5,
        scratch_shapes=[
            pltpu.SMEM((heads,), jnp.int32),
            pltpu.VMEM((heads, dim), f32),
            pltpu.VMEM((1, slab), jnp.int32),
            pltpu.VMEM((1, slab), f32),
        ]
        + [wide] * 4
        + [wide32, wide, wide32, wide32]
        + [
            pltpu.VMEM((heads, slab, slab), bf16),
            pltpu.VMEM((slab, slab), bf16),
            pltpu.VMEM((heads, slab // blk, blk, blk), f32),
            pltpu.VMEM((heads, slab, dim), f32),
            pltpu.VMEM((heads, slab, dim), f32),
            pltpu.VMEM((slab, dim), f32),
            pltpu.VMEM((slab, dim), f32),
            states,
            states,
            states,
            states,
            pltpu.VMEM((heads, dim, dim), f32),
            pltpu.VMEM((heads, dim, dim), bf16),
            pltpu.VMEM((n_head, 2, slab), f32),
            pltpu.VMEM((stages + 2, heads, dim), f32),
            pltpu.VMEM((stages + 1, heads, dim), f32),
            dma((4,)),
            dma((4,)),
            dma((stages, heads)),
            dma((stages, heads)),
            dma((stages, heads)),
            dma((stages, heads)),
            dma((max(n_head - 1, 1),)),
            dma((max(n_head - 1, 1),)),
            dma((stages + 1,)),
            dma((stages + 1,)),
        ],
        compiler_params=pltpu.CompilerParams(
            collective_id=0, has_side_effects=True, vmem_limit_bytes=48 << 20
        ),
        name="lightning",
    )(
        stay(decay_index),
        advantage,
        lengths,
        stay(norm_gain.reshape(heads, dim)),
        stay(loss_mask),
        stay(importance),
        stay(query_rows),
        stay(key_rows),
        stay(value_rows),
        stay(cotangent),
    )
    shapes = tuple(jax.ShapeDtypeStruct(r.shape, r.dtype) for r in results)
    any_space = pl.BlockSpec(memory_space=pl.ANY)
    mixed, dq, dk, dv, gain_grad = pl.pallas_call(
        functools.partial(writer, len(shapes)),
        out_shape=shapes,
        in_specs=[vmem] * len(shapes),
        out_specs=(any_space,) * len(shapes),
        scratch_shapes=[dma((len(shapes),))],
        compiler_params=pltpu.CompilerParams(vmem_limit_bytes=8 << 20),
        name="writer",
    )(*results)
    return (mixed, dq, dk, dv, gain_grad.reshape(features))


def solution(mesh):
    wide = P("dp", "seq", "head")
    token = P("dp", "seq")
    in_specs = (wide, wide, wide, P("head"), wide, token, token, P("dp"), P("dp"), P("head"))
    out_specs = (wide, wide, wide, wide, P("head"))
    body = functools.partial(on_device, mesh.shape["seq"], mesh.shape["head"], mesh.shape["dp"])
    return jax.shard_map(
        body, mesh=mesh, in_specs=in_specs, out_specs=out_specs, check_vma=False
    )
```

profile of v0, /device:TPU:1, one launch (start us, length us, event | category | flops | bytes accessed | tf_op | source)
XLA Modules:
  0.0 49.1 jit_solution(9504408903047888413)
XLA Ops:
  1.9 45.1 %lightning.1 = (bf16[1,512,1024]{2,1,0:T(8,128)(2,1)S(1)}, bf16[1,512,1024]{2,1,0:T(8,128)(2,1)S(1)}, bf16[1,512,1024]{2,1,0:T(8,128)(2,1)S(1)}, bf16[1,512,1024]{2,1,0:T(8,128)(2,1)S(1)}, f32[8,128]{1,0:T(8,128)S(1)}) custom-call(s32[8]{0:T(128)} %decay_hbm.1, f32[1]{0:T(128)S(6)} %copy.15.adv_ref, s32[1]{0:T(128)S(6)} %copy.16.len_ref, f32[8,128]{1,0:T(8,128)} %bitcast.2, ...), custom_call_target="tpu_custom_call" | custom-call | tf_op jit(solution)/shard_map/lightning/pallas_call | solution.py:444
  47.1 2.1 %writer.1 = (bf16[1,512,1024]{2,1,0:T(8,128)(2,1)}, bf16[1,512,1024]{2,1,0:T(8,128)(2,1)}, bf16[1,512,1024]{2,1,0:T(8,128)(2,1)}, bf16[1,512,1024]{2,1,0:T(8,128)(2,1)}, f32[8,128]{1,0:T(8,128)}) custom-call(bf16[1,512,1024]{2,1,0:T(8,128)(2,1)S(1)} %get-tuple-element.15.refs_0_, bf16[1,512,1024]{2,1,0:T(8,128)(2,1)S(1)} %get-tuple-element.16.refs_1_, ...), custom_call_target="tpu_custom_call" | custom-call | tf_op jit(solution)/shard_map/writer/pallas_call | solution.py:503
where the time goes:
time: 49.4 us; the launch traced here: 49.1 us
  Pallas kernels  47.2 us (96%)
  between operations  1.93 us (4%)
    pallas_call x1, Pallas kernels, on_device(): pl.pallas_call(functools.partial(kernel, n_seq, n_head, n_dp), out_shape=...  45.1 us
    pallas_call x1, Pallas kernels, on_device(): pl.pallas_call(functools.partial(writer, len(shapes)), out_shape=shapes,...  2.05 us

commit v1 on v0

v1 whole, which is shorter than its diff:
```python
import functools

import jax
import jax.numpy as jnp
from jax import lax
from jax.experimental import pallas as pl
from jax.experimental.pallas import tpu as pltpu
from jax.sharding import PartitionSpec as P

clip_high = 1.28
epsilon = 1e-06
f32 = jnp.float32
bf16 = jnp.bfloat16
MESH = pl.DeviceIdType.MESH
TURN = 3


def dot(a, b, ca, cb):
    return lax.dot_general(a, b, (((ca,), (cb,)), ((), ())), preferred_element_type=f32)


def kernel(
    n_seq,
    n_head,
    n_dp,
    decay_hbm,
    adv_ref,
    len_ref,
    gain_hbm,
    mask_hbm,
    imp_hbm,
    q_hbm,
    k_hbm,
    v_hbm,
    c_hbm,
    o_mix,
    o_dq,
    o_dk,
    o_dv,
    gg_ref,
    decay_ref,
    gain_ref,
    mask_ref,
    imp_ref,
    q,
    k,
    v,
    c,
    out,
    go,
    pk,
    pv,
    probs0,
    probs1,
    dsc0,
    dsc1,
    wtab0,
    wtab1,
    up,
    down,
    squares,
    mixes,
    tot_f,
    rcv_f,
    tot_b,
    rcv_b,
    pref_f,
    pref_b,
    state,
    stat,
    gsum,
    grcv,
    in_sem,
    kv_sem,
    small_sem,
    fs_sem,
    fr_sem,
    bs_sem,
    br_sem,
    ss_sem,
    sr_sem,
    gs_sem,
    gr_sem,
    turn,
):
    slab, features = q.shape
    heads = decay_ref.shape[0]
    pairs = heads // 2
    dim = features // heads
    blk = min(256, slab)
    nblk = slab // blk
    stages = n_seq.bit_length() - 1
    square = stages == 2
    probs = (probs0, probs1)
    dsc = (dsc0, dsc1)
    wtab = (wtab0, wtab1)
    me = lax.axis_index("seq")
    mh = lax.axis_index("head")
    md = lax.axis_index("dp")
    back = n_seq - 1 - me
    forward = (tot_f, rcv_f, fs_sem, fr_sem, pref_f, me)
    backward = (tot_b, rcv_b, bs_sem, br_sem, pref_b, back)

    def partner(step):
        g = 1 << step
        bit = lax.rem(lax.div(me, g), 2)
        return me + g * (1 - 2 * bit)

    def kv_load(i, which):
        src, dst = ((k_hbm, k), (v_hbm, v))[which]
        span = pl.ds(pl.multiple_of(i * 2 * dim, 2 * dim), 2 * dim)
        return pltpu.make_async_copy(src.at[0, :, span], dst.at[:, span], kv_sem.at[which, i])

    loads = [
        pltpu.make_async_copy(src.at[0], dst, in_sem.at[i])
        for i, (src, dst) in enumerate(((q_hbm, q), (c_hbm, c)))
    ]
    small = [
        pltpu.make_async_copy(src, dst, small_sem.at[i])
        for i, (src, dst) in enumerate(
            (
                (decay_hbm, decay_ref),
                (gain_hbm, gain_ref),
                (mask_hbm, mask_ref),
                (imp_hbm, imp_ref),
            )
        )
    ]
    small[0].start()
    for i in range(pairs):
        kv_load(i, 0).start()
        kv_load(i, 1).start()
    for load in small[1:]:
        load.start()

    barrier = pltpu.get_barrier_semaphore()
    for s in range(stages):
        pl.semaphore_signal(barrier, inc=1, device_id={"seq": partner(s)}, device_id_type=MESH)
    for off in range(1, n_head):
        pl.semaphore_signal(
            barrier, inc=1, device_id={"head": lax.rem(mh + off, n_head)}, device_id_type=MESH
        )
    for off in range(1, n_dp):
        pl.semaphore_signal(
            barrier, inc=1, device_id={"dp": lax.rem(md + off, n_dp)}, device_id_type=MESH
        )

    def cols(h):
        return pl.ds(pl.multiple_of(h * dim, dim), dim)

    def rate(h, width):
        index = jnp.full((1, width), decay_ref[h], jnp.int32).astype(f32)
        return 16.0 / (slab * jnp.exp2(index))

    small[0].wait()
    base = min(128, slab)
    line = lax.broadcasted_iota(jnp.int32, (base, dim), 0).astype(f32)

    @pl.loop(0, heads)
    def _(h):
        r = rate(h, dim)
        rise = jnp.exp2(-r * line)
        fall = jnp.exp2(-r * (base - 1.0 - line))
        for b in range(slab // base):
            rows = pl.ds(b * base, base)
            up[h, rows, :] = rise * jnp.exp2(-r * float(b * base))
            down[h, rows, :] = fall * jnp.exp2(-r * float(slab - (b + 1) * base))

    def hop(d, s, h, bit, src=None):
        tot, rcv, send, recv, _, _ = d
        return pltpu.make_async_remote_copy(
            src_ref=tot.at[s, h] if src is None else src,
            dst_ref=rcv.at[s, h],
            send_sem=send.at[s, h],
            recv_sem=recv.at[s, h],
            device_id={"seq": partner(bit)},
            device_id_type=MESH,
        )

    def lower_only(s, place):
        return lax.div(place, 2 << s) == n_seq // (2 << s) - 1

    def is_upper(s, place):
        return lax.rem(lax.div(place, 1 << s), 2) == 1

    def sends(s, place):
        return jnp.logical_not(jnp.logical_and(is_upper(s, place), lower_only(s, place)))

    def takes(s, place):
        return jnp.logical_or(is_upper(s, place), jnp.logical_not(lower_only(s, place)))

    def begin(d, s, h):
        @pl.when(sends(s, d[5]))
        def _():
            hop(d, s, h, s).start()

    def accept(d, h, s):
        tot, rcv, _, _, pref, place = d

        @pl.when(takes(s, place))
        def _():
            hop(d, s, h, s).wait_recv()
            g = 1 << s
            r = rate(h, dim) * slab
            upper = jnp.full((1, dim), lax.rem(lax.div(place, g), 2), jnp.int32).astype(f32)
            inner = jnp.full((1, dim), lax.rem(place, g), jnp.int32).astype(f32)
            got = rcv[s, h]
            to_prefix = upper * jnp.exp2(-r * inner)
            if s == 0:
                pref[h] = to_prefix * got
            else:
                pref[h] = pref[h] + to_prefix * got
            if s + 1 < stages:
                whole = jnp.exp2(-r * g)
                from_got = upper * whole + (1.0 - upper)
                from_own = upper + (1.0 - upper) * whole
                tot[s + 1, h] = from_got * got + from_own * tot[s, h]

        if s + 1 < stages:
            begin(d, s + 1, h)

    def begin_pair(d, i):
        place = d[5]
        begin(d, 0, 2 * i)
        if square:

            @pl.when(place < 2)
            def _():
                hop(d, 0, 2 * i + 1, 1).start()
        else:
            begin(d, 0, 2 * i + 1)

    def begin_rest(d):
        if square:
            tot, place = d[0], d[5]

            @pl.when(place == 0)
            def _():
                @pl.loop(0, pairs)
                def _(i):
                    hop(d, 1, 2 * i + 1, 0, tot.at[0, 2 * i + 1]).start()

    def accept_pair(d, i):
        tot, rcv, _, _, pref, place = d
        accept(d, 2 * i, 0)
        h = 2 * i + 1
        if not square:
            accept(d, h, 0)
            return

        @pl.when(place == 3)
        def _():
            hop(d, 0, h, 1).wait_recv()
            hop(d, 1, h, 0, rcv.at[0, h]).start()
            pref[h] = jnp.exp2(-rate(h, dim) * slab) * rcv[0, h]

        @pl.when(place == 2)
        def _():
            hop(d, 0, h, 1).wait_recv()
            fade = jnp.exp2(-rate(h, dim) * slab)
            got = fade * rcv[0, h]
            tot[1, h] = tot[0, h] + fade * got
            pref[h] = got
            hop(d, 1, h, 0).start()

    def finish_pair(d, i):
        _, rcv, _, _, pref, place = d
        if stages > 1:
            accept(d, 2 * i, stages - 1)
        h = 2 * i + 1
        if square:

            @pl.when(place != 0)
            def _():
                hop(d, 1, h, 0).wait_recv()
                pref[h] = pref[h] + rcv[1, h]
        elif stages > 1:
            accept(d, h, stages - 1)

    def middle(d):
        for s in range(1, stages - 1):

            @pl.loop(0, heads)
            def _(h, s=s):
                accept(d, h, s)

    def settle(d):
        place = d[5]
        for s in range(stages):
            for odd in range(2):
                bit = stages - 1 - s if square and odd else s
                if not (square and odd):
                    cond = sends(s, place)
                elif s == 0:
                    cond = place < 2
                else:
                    cond = place != 1

                @pl.when(cond)
                def _(s=s, odd=odd, bit=bit):
                    @pl.loop(0, pairs)
                    def _(i):
                        hop(d, s, 2 * i + odd, bit).wait_send()

    def local(i):
        kv_load(i, 0).wait()
        kv_load(i, 1).wait()
        for odd in range(2):
            h = 2 * i + odd
            faded = (k[:, cols(h)].astype(f32) * down[h]).astype(bf16)
            tot_f[0, h] = dot(faded, v[:, cols(h)], 0, 0)

    local(0)
    for load in loads:
        load.start()
    pl.semaphore_wait(barrier, stages + n_head - 1 + n_dp - 1)
    first = md == 0

    @pl.when(first)
    def _():
        begin_pair(forward, 0)

    @pl.loop(1, pairs)
    def _(i):
        local(i)

        @pl.when(first)
        def _():
            begin_pair(forward, i)

    @pl.when(first)
    def _():
        begin_rest(forward)

    @pl.loop(0, heads)
    def _(h):
        pref_f[h] = jnp.zeros((dim, dim), f32)
        pref_b[h] = jnp.zeros((dim, dim), f32)

    loads[0].wait()

    t_at = lax.broadcasted_iota(jnp.int32, (blk, blk), 0)
    s_at = lax.broadcasted_iota(jnp.int32, (blk, blk), 1)
    shift = min(TURN, pairs - 1)

    @pl.loop(0, pairs)
    def _(i):
        for odd in range(2):
            h = 2 * i + odd
            r = rate(h, dim)
            place = lax.broadcasted_iota(jnp.int32, (1, dim), 1).astype(f32)
            front = up[h, pl.ds(0, blk), :]
            near = jnp.concatenate(
                [front * jnp.exp2(r * (place + float(b * dim))) for b in range(blk // dim)],
                axis=1,
            )
            wtab[odd][i, 0] = jnp.where(t_at >= s_at, near, 0.0)
            for d in range(1, nblk):
                away = jnp.exp2(-r * float(blk * d))
                wtab[odd][i, d] = near * jnp.concatenate([away] * (blk // dim), axis=1)
        for a in range(nblk):
            rows = pl.ds(a * blk, blk)
            for odd in range(2):
                h = 2 * i + odd
                for b in range(a + 1):
                    past = pl.ds(b * blk, blk)
                    score = dot(q[rows, cols(h)], k[past, cols(h)], 1, 1)
                    probs[odd][i, rows, past] = (score * wtab[odd][i, a - b]).astype(bf16)
        for a in range(nblk):
            rows = pl.ds(a * blk, blk)
            past = pl.ds(0, (a + 1) * blk)
            for odd in range(2):
                h = 2 * i + odd
                out[rows, cols(h)] = dot(probs[odd][i, rows, past], v[past, cols(h)], 1, 0)

        if n_dp > 1:

            @pl.when(jnp.logical_and(first, i == shift))
            def _():
                pl.semaphore_signal(turn, inc=1, device_id={"dp": 1 - md}, device_id_type=MESH)

            @pl.when(jnp.logical_and(jnp.logical_not(first), i == shift))
            def _():
                pl.semaphore_wait(turn, 1)

                @pl.loop(0, pairs)
                def _(p):
                    begin_pair(forward, p)

                begin_rest(forward)

        @pl.when(jnp.logical_and(first, i >= 1))
        def _():
            accept_pair(forward, i - 1)

    @pl.when(first)
    def _():
        accept_pair(forward, pairs - 1)

    @pl.when(jnp.logical_not(first))
    def _():
        @pl.loop(0, pairs)
        def _(i):
            accept_pair(forward, i)

    middle(forward)

    loads[1].wait()
    for load in small[1:]:
        load.wait()

    token = mask_ref[...].astype(f32)
    at = me * slab + lax.broadcasted_iota(jnp.int32, (1, slab), 1)
    length = jnp.full((1, slab), len_ref[0], jnp.int32)
    token = token * (at < length).astype(f32) * jnp.minimum(imp_ref[...], clip_high)
    token = token * adv_ref[0] * (float(slab * n_seq) / length.astype(f32))

    squares[...] = jnp.zeros((slab, dim), f32)
    mixes[...] = jnp.zeros((slab, dim), f32)

    @pl.loop(0, pairs)
    def _(i):
        finish_pair(forward, i)
        fulls = []
        for odd in range(2):
            h = 2 * i + odd
            half = pref_f[h].astype(bf16)
            state[h] = half
            grow = up[h] * jnp.exp2(-rate(h, dim))
            full = out[:, cols(h)] + dot(q[:, cols(h)], half, 1, 0) * grow
            out[:, cols(h)] = full
            fulls.append((full, c[:, cols(h)].astype(f32) * gain_ref[pl.ds(h, 1), :] * full))
        squares[...] += fulls[0][0] * fulls[0][0] + fulls[1][0] * fulls[1][0]
        mixes[...] += fulls[0][1] + fulls[1][1]

    stat[mh, 0:1, :] = jnp.sum(squares[...].T, axis=0, keepdims=True)
    stat[mh, 1:2, :] = jnp.sum(mixes[...].T, axis=0, keepdims=True) * token
    posts = [
        pltpu.make_async_remote_copy(
            src_ref=stat.at[mh],
            dst_ref=stat.at[mh],
            send_sem=ss_sem.at[off - 1],
            recv_sem=sr_sem.at[off - 1],
            device_id={"head": lax.rem(mh + off, n_head)},
            device_id_type=MESH,
        )
        for off in range(1, n_head)
    ]
    for post in posts:
        post.start()
    settle(forward)
    for post in posts:
        post.wait()
    sums = stat[0]
    for i in range(1, n_head):
        sums = sums + stat[i]
    count = features * n_head
    inverse = lax.rsqrt(sums[0:1] / count + epsilon)
    mean = inverse * (sums[1:2] / count)

    def column(row):
        return jnp.broadcast_to(row, (dim, slab)).T

    inv_col = column(inverse)
    give_col = column(inverse * token)
    take_col = column(inverse * inverse * mean)

    @pl.loop(0, pairs)
    def _(i):
        for odd in range(2):
            h = 2 * i + odd
            gain = gain_ref[pl.ds(h, 1), :]
            given = c[:, cols(h)].astype(f32) * give_col
            grad = (given * gain - take_col * out[:, cols(h)]).astype(bf16)
            go[:, cols(h)] = grad
            faded = (q[:, cols(h)].astype(f32) * up[h]).astype(bf16)
            tot_b[0, h] = dot(faded, grad, 0, 0)
        begin_pair(backward, i)

    begin_rest(backward)

    @pl.loop(0, heads)
    def _(h):
        gain = gain_ref[pl.ds(h, 1), :]
        full = out[:, cols(h)]
        given = c[:, cols(h)].astype(f32) * give_col
        o_mix[0, :, cols(h)] = (full * inv_col * gain).astype(bf16)
        gsum[0, pl.ds(h, 1), :] = jnp.sum(given * full, axis=0, keepdims=True)

    def gain_copy(s):
        target = {"dp": lax.rem(md + 1, n_dp)} if s == stages else {"seq": partner(s)}
        return pltpu.make_async_remote_copy(
            src_ref=gsum.at[s],
            dst_ref=grcv.at[s],
            send_sem=gs_sem.at[s],
            recv_sem=gr_sem.at[s],
            device_id=target,
            device_id_type=MESH,
        )

    rounds = stages + (1 if n_dp > 1 else 0)

    def gain_round(s):
        gain_copy(s).wait()
        gsum[s + 1] = gsum[s] + grcv[s]
        if s + 1 < rounds:
            gain_copy(s + 1).start()

    gain_copy(0).start()

    @pl.loop(0, pairs)
    def _(i):
        for a in range(nblk):
            rows = pl.ds(a * blk, blk)
            for odd in range(2):
                h = 2 * i + odd
                grad = go[rows, cols(h)]
                for b in range(a + 1):
                    past = pl.ds(b * blk, blk)
                    score = dot(grad, v[past, cols(h)], 1, 1)
                    dsc[odd][rows, past] = (score * wtab[odd][i, a - b]).astype(bf16)
        for a in range(nblk):
            rows = pl.ds(a * blk, blk)
            past = pl.ds(0, (a + 1) * blk)
            for odd in range(2):
                h = 2 * i + odd
                grow = up[h, rows, :] * jnp.exp2(-rate(h, dim))
                total = dot(dsc[odd][rows, past], k[past, cols(h)], 1, 0)
                total = total + dot(go[rows, cols(h)], state[h], 1, 1) * grow
                o_dq[0, rows, cols(h)] = total.astype(bf16)
        for b in range(nblk):
            past = pl.ds(b * blk, blk)
            rest = pl.ds(b * blk, slab - b * blk)
            for odd in range(2):
                h = 2 * i + odd
                pk[past, cols(h)] = dot(dsc[odd][rest, past], q[rest, cols(h)], 0, 0)
                pv[past, cols(h)] = dot(probs[odd][i, rest, past], go[rest, cols(h)], 0, 0)

        @pl.when(2 * i < pairs)
        def _():
            accept_pair(backward, 2 * i)

        @pl.when(2 * i + 1 < pairs)
        def _():
            accept_pair(backward, 2 * i + 1)

        @pl.when(i == pairs // 2)
        def _():
            gain_round(0)

    for s in range(1, rounds - 1):
        gain_round(s)
    middle(backward)

    @pl.loop(0, pairs)
    def _(i):
        finish_pair(backward, i)
        for odd in range(2):
            h = 2 * i + odd
            half = pref_b[h].astype(bf16)
            fade = down[h] * jnp.exp2(-rate(h, dim))
            dk = pk[:, cols(h)] + dot(v[:, cols(h)], half, 1, 1) * fade
            o_dk[0, :, cols(h)] = dk.astype(bf16)
            dv = pv[:, cols(h)] + dot(k[:, cols(h)], half, 1, 0) * fade
            o_dv[0, :, cols(h)] = dv.astype(bf16)

    if rounds > 1:
        gain_round(rounds - 1)
    gg_ref[...] = gsum[rounds]
    settle(backward)


def writer(n, *refs):
    sem = refs[-1]
    copies = [pltpu.make_async_copy(refs[i], refs[n + i], sem.at[i]) for i in range(n)]
    for copy in copies:
        copy.start()
    for copy in copies:
        copy.wait()


def on_device(
    n_seq,
    n_head,
    n_dp,
    query_rows,
    key_rows,
    value_rows,
    norm_gain,
    cotangent,
    loss_mask,
    importance,
    advantage,
    lengths,
    decay_index,
):
    batches, slab, features = query_rows.shape
    heads = decay_index.shape[0]
    dim = features // heads
    stages = n_seq.bit_length() - 1
    assert batches == 1 and heads % 2 == 0 and n_seq == 1 << stages and stages > 0 and n_dp <= 2
    vmem = pl.BlockSpec(memory_space=pltpu.VMEM)
    smem = pl.BlockSpec(memory_space=pltpu.SMEM)
    far = pl.BlockSpec(memory_space=pltpu.HBM)
    rows = jax.ShapeDtypeStruct(query_rows.shape, bf16)
    wide = pltpu.VMEM((slab, features), bf16)
    wide32 = pltpu.VMEM((slab, features), f32)
    blk = min(256, slab)
    states = pltpu.VMEM((stages, heads, dim, dim), f32)
    dma = pltpu.SemaphoreType.DMA

    def stay(array):
        return pltpu.with_memory_space_constraint(array, pltpu.HBM)

    results = pl.pallas_call(
        functools.partial(kernel, n_seq, n_head, n_dp),
        out_shape=(rows, rows, rows, rows, jax.ShapeDtypeStruct((heads, dim), f32)),
        in_specs=[far, smem, smem] + [far] * 7,
        out_specs=(vmem,) * 5,
        scratch_shapes=[
            pltpu.SMEM((heads,), jnp.int32),
            pltpu.VMEM((heads, dim), f32),
            pltpu.VMEM((1, slab), jnp.int32),
            pltpu.VMEM((1, slab), f32),
        ]
        + [wide] * 4
        + [wide32, wide, wide32, wide32]
        + [
            pltpu.VMEM((heads // 2, slab, slab), bf16),
            pltpu.VMEM((heads // 2, slab, slab), bf16),
            pltpu.VMEM((slab, slab), bf16),
            pltpu.VMEM((slab, slab), bf16),
            pltpu.VMEM((heads // 2, slab // blk, blk, blk), f32),
            pltpu.VMEM((heads // 2, slab // blk, blk, blk), f32),
            pltpu.VMEM((heads, slab, dim), f32),
            pltpu.VMEM((heads, slab, dim), f32),
            pltpu.VMEM((slab, dim), f32),
            pltpu.VMEM((slab, dim), f32),
            states,
            states,
            states,
            states,
            pltpu.VMEM((heads, dim, dim), f32),
            pltpu.VMEM((heads, dim, dim), f32),
            pltpu.VMEM((heads, dim, dim), bf16),
            pltpu.VMEM((n_head, 2, slab), f32),
            pltpu.VMEM((stages + 2, heads, dim), f32),
            pltpu.VMEM((stages + 1, heads, dim), f32),
            dma((2,)),
            dma((2, heads // 2)),
            dma((4,)),
            dma((stages, heads)),
            dma((stages, heads)),
            dma((stages, heads)),
            dma((stages, heads)),
            dma((max(n_head - 1, 1),)),
            dma((max(n_head - 1, 1),)),
            dma((stages + 1,)),
            dma((stages + 1,)),
            pltpu.SemaphoreType.REGULAR,
        ],
        compiler_params=pltpu.CompilerParams(
            collective_id=0, has_side_effects=True, vmem_limit_bytes=48 << 20
        ),
        name="lightning",
    )(
        stay(decay_index),
        advantage,
        lengths,
        stay(norm_gain.reshape(heads, dim)),
        stay(loss_mask),
        stay(importance),
        stay(query_rows),
        stay(key_rows),
        stay(value_rows),
        stay(cotangent),
    )
    shapes = tuple(jax.ShapeDtypeStruct(r.shape, r.dtype) for r in results)
    any_space = pl.BlockSpec(memory_space=pl.ANY)
    mixed, dq, dk, dv, gain_grad = pl.pallas_call(
        functools.partial(writer, len(shapes)),
        out_shape=shapes,
        in_specs=[vmem] * len(shapes),
        out_specs=(any_space,) * len(shapes),
        scratch_shapes=[dma((len(shapes),))],
        compiler_params=pltpu.CompilerParams(vmem_limit_bytes=8 << 20),
        name="writer",
    )(*results)
    return (mixed, dq, dk, dv, gain_grad.reshape(features))


def solution(mesh):
    wide = P("dp", "seq", "head")
    token = P("dp", "seq")
    in_specs = (wide, wide, wide, P("head"), wide, token, token, P("dp"), P("dp"), P("head"))
    out_specs = (wide, wide, wide, wide, P("head"))
    body = functools.partial(on_device, mesh.shape["seq"], mesh.shape["head"], mesh.shape["dp"])
    return jax.shard_map(
        body, mesh=mesh, in_specs=in_specs, out_specs=out_specs, check_vma=False
    )
```

time: 49.4 us -> 41.6 us (0.84)
  Pallas kernels: 47.2 us -> 39.5 us
    pallas_call x1, Pallas kernels: 45.1 us -> 37.5 us  [on_device(): pl.pallas_call(functools.partial(kernel, n_seq, n_head, n_dp), out_shape=...]
where the time goes in v1:
time: 41.6 us; the launch traced here: 41.5 us
  Pallas kernels  39.5 us (95%)
  between operations  1.93 us (5%)
    pallas_call x1, Pallas kernels, on_device(): pl.pallas_call(functools.partial(kernel, n_seq, n_head, n_dp), out_shape=...  37.5 us
    pallas_call x1, Pallas kernels, on_device(): pl.pallas_call(functools.partial(writer, len(shapes)), out_shape=shapes,...  2.05 us

profile of v1, /device:TPU:1, one launch (start us, length us, event | category | flops | bytes accessed | tf_op | source)
XLA Modules:
  0.0 41.5 jit_solution(17749696534992859364)
XLA Ops:
  1.9 37.5 %lightning.1 = (bf16[1,512,1024]{2,1,0:T(8,128)(2,1)S(1)}, bf16[1,512,1024]{2,1,0:T(8,128)(2,1)S(1)}, bf16[1,512,1024]{2,1,0:T(8,128)(2,1)S(1)}, bf16[1,512,1024]{2,1,0:T(8,128)(2,1)S(1)}, f32[8,128]{1,0:T(8,128)S(1)}) custom-call(s32[8]{0:T(128)} %decay_hbm.1, f32[1]{0:T(128)S(6)} %copy.15.adv_ref, s32[1]{0:T(128)S(6)} %copy.16.len_ref, f32[8,128]{1,0:T(8,128)} %bitcast.2, ...), custom_call_target="tpu_custom_call" | custom-call | tf_op jit(solution)/shard_map/lightning/pallas_call | solution.py:615
  39.4 2.1 %writer.1 = (bf16[1,512,1024]{2,1,0:T(8,128)(2,1)}, bf16[1,512,1024]{2,1,0:T(8,128)(2,1)}, bf16[1,512,1024]{2,1,0:T(8,128)(2,1)}, bf16[1,512,1024]{2,1,0:T(8,128)(2,1)}, f32[8,128]{1,0:T(8,128)}) custom-call(bf16[1,512,1024]{2,1,0:T(8,128)(2,1)S(1)} %get-tuple-element.15.refs_0_, bf16[1,512,1024]{2,1,0:T(8,128)(2,1)S(1)} %get-tuple-element.16.refs_1_, ...), custom_call_target="tpu_custom_call" | custom-call | tf_op jit(solution)/shard_map/writer/pallas_call | solution.py:680

commit v2 on v1

--- a/solution.py
+++ b/solution.py
@@ -69,7 +69,7 @@
     state,
     stat,
     gsum,
-    grcv,
+    gpair,
     in_sem,
     kv_sem,
     small_sem,
@@ -127,15 +127,14 @@
         )
     ]
     small[0].start()
-    for i in range(pairs):
-        kv_load(i, 0).start()
-        kv_load(i, 1).start()
-    for load in small[1:]:
-        load.start()
+    kv_load(0, 0).start()
+    kv_load(0, 1).start()
 
     barrier = pltpu.get_barrier_semaphore()
-    for s in range(stages):
-        pl.semaphore_signal(barrier, inc=1, device_id={"seq": partner(s)}, device_id_type=MESH)
+    for off in range(1, n_seq):
+        pl.semaphore_signal(
+            barrier, inc=1, device_id={"seq": lax.rem(me + off, n_seq)}, device_id_type=MESH
+        )
     for off in range(1, n_head):
         pl.semaphore_signal(
             barrier, inc=1, device_id={"head": lax.rem(mh + off, n_head)}, device_id_type=MESH
@@ -145,6 +144,12 @@
             barrier, inc=1, device_id={"dp": lax.rem(md + off, n_dp)}, device_id_type=MESH
         )
 
+    for i in range(1, pairs):
+        kv_load(i, 0).start()
+        kv_load(i, 1).start()
+    for load in small[1:]:
+        load.start()
+
     def cols(h):
         return pl.ds(pl.multiple_of(h * dim, dim), dim)
 
@@ -156,15 +161,19 @@
     base = min(128, slab)
     line = lax.broadcasted_iota(jnp.int32, (base, dim), 0).astype(f32)
 
-    @pl.loop(0, heads)
-    def _(h):
+    def falling(h):
         r = rate(h, dim)
-        rise = jnp.exp2(-r * line)
         fall = jnp.exp2(-r * (base - 1.0 - line))
         for b in range(slab // base):
             rows = pl.ds(b * base, base)
+            down[h, rows, :] = fall * jnp.exp2(-r * float(slab - (b + 1) * base))
+
+    def rising(h):
+        r = rate(h, dim)
+        rise = jnp.exp2(-r * line)
+        for b in range(slab // base):
+            rows = pl.ds(b * base, base)
             up[h, rows, :] = rise * jnp.exp2(-r * float(b * base))
-            down[h, rows, :] = fall * jnp.exp2(-r * float(slab - (b + 1) * base))
 
     def hop(d, s, h, bit, src=None):
         tot, rcv, send, recv, _, _ = d
@@ -219,9 +228,11 @@
         if s + 1 < stages:
             begin(d, s + 1, h)
 
-    def begin_pair(d, i):
+    def begin_even(d, i):
+        begin(d, 0, 2 * i)
+
+    def begin_odd(d, i):
         place = d[5]
-        begin(d, 0, 2 * i)
         if square:
 
             @pl.when(place < 2)
@@ -229,6 +240,10 @@
                 hop(d, 0, 2 * i + 1, 1).start()
         else:
             begin(d, 0, 2 * i + 1)
+
+    def begin_pair(d, i):
+        begin_even(d, i)
+        begin_odd(d, i)
 
     def begin_rest(d):
         if square:
@@ -263,10 +278,12 @@
             pref[h] = got
             hop(d, 1, h, 0).start()
 
-    def finish_pair(d, i):
-        _, rcv, _, _, pref, place = d
+    def finish_even(d, i):
         if stages > 1:
             accept(d, 2 * i, stages - 1)
+
+    def finish_odd(d, i):
+        _, rcv, _, _, pref, place = d
         h = 2 * i + 1
         if square:
 
@@ -303,6 +320,8 @@
                         hop(d, s, 2 * i + odd, bit).wait_send()
 
     def local(i):
+        falling(2 * i)
+        falling(2 * i + 1)
         kv_load(i, 0).wait()
         kv_load(i, 1).wait()
         for odd in range(2):
@@ -313,7 +332,7 @@
     local(0)
     for load in loads:
         load.start()
-    pl.semaphore_wait(barrier, stages + n_head - 1 + n_dp - 1)
+    pl.semaphore_wait(barrier, n_seq - 1 + n_head - 1 + n_dp - 1)
     first = md == 0
 
     @pl.when(first)
@@ -334,6 +353,7 @@
 
     @pl.loop(0, heads)
     def _(h):
+        rising(h)
         pref_f[h] = jnp.zeros((dim, dim), f32)
         pref_b[h] = jnp.zeros((dim, dim), f32)
 
@@ -373,6 +393,12 @@
                 h = 2 * i + odd
                 out[rows, cols(h)] = dot(probs[odd][i, rows, past], v[past, cols(h)], 1, 0)
 
+        for ahead in (1, 0):
+
+            @pl.when(jnp.logical_and(first, (2 * i - ahead >= 0) & (2 * i - ahead < pairs)))
+            def _(ahead=ahead):
+                accept_pair(forward, 2 * i - ahead)
+
         if n_dp > 1:
 
             @pl.when(jnp.logical_and(first, i == shift))
@@ -388,14 +414,6 @@
                     begin_pair(forward, p)
 
                 begin_rest(forward)
-
-        @pl.when(jnp.logical_and(first, i >= 1))
-        def _():
-            accept_pair(forward, i - 1)
-
-    @pl.when(first)
-    def _():
-        accept_pair(forward, pairs - 1)
 
     @pl.when(jnp.logical_not(first))
     def _():
@@ -418,20 +436,31 @@
     squares[...] = jnp.zeros((slab, dim), f32)
     mixes[...] = jnp.zeros((slab, dim), f32)
 
-    @pl.loop(0, pairs)
+    def widen(h):
+        half = pref_f[h].astype(bf16)
+        state[h] = half
+        grow = up[h] * jnp.exp2(-rate(h, dim))
+        full = out[:, cols(h)] + dot(q[:, cols(h)], half, 1, 0) * grow
+        out[:, cols(h)] = full
+        return full, c[:, cols(h)].astype(f32) * gain_ref[pl.ds(h, 1), :] * full
+
+    @pl.loop(0, pairs - 1)
     def _(i):
-        finish_pair(forward, i)
-        fulls = []
-        for odd in range(2):
-            h = 2 * i + odd
-            half = pref_f[h].astype(bf16)
-            state[h] = half
-            grow = up[h] * jnp.exp2(-rate(h, dim))
-            full = out[:, cols(h)] + dot(q[:, cols(h)], half, 1, 0) * grow
-            out[:, cols(h)] = full
-            fulls.append((full, c[:, cols(h)].astype(f32) * gain_ref[pl.ds(h, 1), :] * full))
-        squares[...] += fulls[0][0] * fulls[0][0] + fulls[1][0] * fulls[1][0]
-        mixes[...] += fulls[0][1] + fulls[1][1]
+        finish_even(forward, i)
+        finish_odd(forward, i)
+        full, mix = widen(2 * i)
+        other, blend = widen(2 * i + 1)
+        squares[...] += full * full + other * other
+        mixes[...] += mix + blend
+
+    finish_even(forward, pairs - 1)
+    full, mix = widen(heads - 2)
+    squares[...] += full * full
+    mixes[...] += mix
+    finish_odd(forward, pairs - 1)
+    full, mix = widen(heads - 1)
+    squares[...] += full * full
+    mixes[...] += mix
 
     stat[mh, 0:1, :] = jnp.sum(squares[...].T, axis=0, keepdims=True)
     stat[mh, 1:2, :] = jnp.sum(mixes[...].T, axis=0, keepdims=True) * token
@@ -448,9 +477,8 @@
     ]
     for post in posts:
         post.start()
-    settle(forward)
     for post in posts:
-        post.wait()
+        post.wait_recv()
     sums = stat[0]
     for i in range(1, n_head):
         sums = sums + stat[i]
@@ -465,17 +493,24 @@
     give_col = column(inverse * token)
     take_col = column(inverse * inverse * mean)
 
-    @pl.loop(0, pairs)
+    def give(h):
+        given = c[:, cols(h)].astype(f32) * give_col
+        grad = (given * gain_ref[pl.ds(h, 1), :] - take_col * out[:, cols(h)]).astype(bf16)
+        go[:, cols(h)] = grad
+        faded = (q[:, cols(h)].astype(f32) * up[h]).astype(bf16)
+        tot_b[0, h] = dot(faded, grad, 0, 0)
+
+    give(0)
+    begin_even(backward, 0)
+    give(1)
+    begin_odd(backward, 0)
+
+    @pl.loop(1, pairs)
     def _(i):
-        for odd in range(2):
-            h = 2 * i + odd
-            gain = gain_ref[pl.ds(h, 1), :]
-            given = c[:, cols(h)].astype(f32) * give_col
-            grad = (given * gain - take_col * out[:, cols(h)]).astype(bf16)
-            go[:, cols(h)] = grad
-            faded = (q[:, cols(h)].astype(f32) * up[h]).astype(bf16)
-            tot_b[0, h] = dot(faded, grad, 0, 0)
-        begin_pair(backward, i)
+        give(2 * i)
+        give(2 * i + 1)
+        begin_even(backward, i)
+        begin_odd(backward, i)
 
     begin_rest(backward)
 
@@ -485,28 +520,30 @@
         full = out[:, cols(h)]
         given = c[:, cols(h)].astype(f32) * give_col
         o_mix[0, :, cols(h)] = (full * inv_col * gain).astype(bf16)
-        gsum[0, pl.ds(h, 1), :] = jnp.sum(given * full, axis=0, keepdims=True)
-
-    def gain_copy(s):
-        target = {"dp": lax.rem(md + 1, n_dp)} if s == stages else {"seq": partner(s)}
-        return pltpu.make_async_remote_copy(
-            src_ref=gsum.at[s],
-            dst_ref=grcv.at[s],
-            send_sem=gs_sem.at[s],
-            recv_sem=gr_sem.at[s],
-            device_id=target,
+        gsum[me, pl.ds(h, 1), :] = jnp.sum(given * full, axis=0, keepdims=True)
+
+    shares = [
+        pltpu.make_async_remote_copy(
+            src_ref=gsum.at[me],
+            dst_ref=gsum.at[me],
+            send_sem=gs_sem.at[off],
+            recv_sem=gr_sem.at[off],
+            device_id={"seq": lax.rem(me + off, n_seq)},
             device_id_type=MESH,
         )
-
-    rounds = stages + (1 if n_dp > 1 else 0)
-
-    def gain_round(s):
-        gain_copy(s).wait()
-        gsum[s + 1] = gsum[s] + grcv[s]
-        if s + 1 < rounds:
-            gain_copy(s + 1).start()
-
-    gain_copy(0).start()
+        for off in range(1, n_seq)
+    ]
+    swap = pltpu.make_async_remote_copy(
+        src_ref=gpair.at[0],
+        dst_ref=gpair.at[1],
+        send_sem=gs_sem.at[0],
+        recv_sem=gr_sem.at[0],
+        device_id={"dp": lax.rem(md + 1, n_dp)},
+        device_id_type=MESH,
+    )
+    for share in shares:
+        share.start()
+    accept_pair(backward, 0)
 
     @pl.loop(0, pairs)
     def _(i):
@@ -536,37 +573,49 @@
                 pk[past, cols(h)] = dot(dsc[odd][rest, past], q[rest, cols(h)], 0, 0)
                 pv[past, cols(h)] = dot(probs[odd][i, rest, past], go[rest, cols(h)], 0, 0)
 
-        @pl.when(2 * i < pairs)
-        def _():
-            accept_pair(backward, 2 * i)
-
-        @pl.when(2 * i + 1 < pairs)
-        def _():
-            accept_pair(backward, 2 * i + 1)
-
-        @pl.when(i == pairs // 2)
-        def _():
-            gain_round(0)
-
-    for s in range(1, rounds - 1):
-        gain_round(s)
+        for ahead in (1, 2):
+
+            @pl.when(2 * i + ahead < pairs)
+            def _(ahead=ahead):
+                accept_pair(backward, 2 * i + ahead)
+
+    for share in shares:
+        share.wait_recv()
+    total = gsum[0]
+    for s in range(1, n_seq):
+        total = total + gsum[s]
+    gpair[0] = total
+    if n_dp > 1:
+        swap.start()
     middle(backward)
 
-    @pl.loop(0, pairs)
+    def close(h):
+        half = pref_b[h].astype(bf16)
+        fade = down[h] * jnp.exp2(-rate(h, dim))
+        dk = pk[:, cols(h)] + dot(v[:, cols(h)], half, 1, 1) * fade
+        o_dk[0, :, cols(h)] = dk.astype(bf16)
+        dv = pv[:, cols(h)] + dot(k[:, cols(h)], half, 1, 0) * fade
+        o_dv[0, :, cols(h)] = dv.astype(bf16)
+
+    @pl.loop(0, pairs - 1)
     def _(i):
-        finish_pair(backward, i)
-        for odd in range(2):
-            h = 2 * i + odd
-            half = pref_b[h].astype(bf16)
-            fade = down[h] * jnp.exp2(-rate(h, dim))
-            dk = pk[:, cols(h)] + dot(v[:, cols(h)], half, 1, 1) * fade
-            o_dk[0, :, cols(h)] = dk.astype(bf16)
-            dv = pv[:, cols(h)] + dot(k[:, cols(h)], half, 1, 0) * fade
-            o_dv[0, :, cols(h)] = dv.astype(bf16)
-
-    if rounds > 1:
-        gain_round(rounds - 1)
-    gg_ref[...] = gsum[rounds]
+        finish_even(backward, i)
+        finish_odd(backward, i)
+        close(2 * i)
+        close(2 * i + 1)
+
+    finish_even(backward, pairs - 1)
+    close(heads - 2)
+    finish_odd(backward, pairs - 1)
+    close(heads - 1)
+    if n_dp > 1:
+        swap.wait()
+        gg_ref[...] = gpair[0] + gpair[1]
+    else:
+        gg_ref[...] = gpair[0]
+    for post in posts + shares:
+        post.wait_send()
+    settle(forward)
     settle(backward)
 
 
@@ -644,8 +693,8 @@
             pltpu.VMEM((heads, dim, dim), f32),
             pltpu.VMEM((heads, dim, dim), bf16),
             pltpu.VMEM((n_head, 2, slab), f32),
-            pltpu.VMEM((stages + 2, heads, dim), f32),
-            pltpu.VMEM((stages + 1, heads, dim), f32),
+            pltpu.VMEM((n_seq, heads, dim), f32),
+            pltpu.VMEM((2, heads, dim), f32),
             dma((2,)),
             dma((2, heads // 2)),
             dma((4,)),
@@ -655,8 +704,8 @@
             dma((stages, heads)),
             dma((max(n_head - 1, 1),)),
             dma((max(n_head - 1, 1),)),
-            dma((stages + 1,)),
-            dma((stages + 1,)),
+            dma((n_seq,)),
+            dma((n_seq,)),
             pltpu.SemaphoreType.REGULAR,
         ],
         compiler_params=pltpu.CompilerParams(

time: 41.6 us -> 39.8 us (0.957)
  Pallas kernels: 39.5 us -> 37.7 us
    pallas_call x1, Pallas kernels: 37.5 us -> 35.6 us  [on_device(): pl.pallas_call(functools.partial(kernel, n_seq, n_head, n_dp), out_shape=...]
where the time goes in v2:
time: 39.8 us; the launch traced here: 39.6 us
  Pallas kernels  37.7 us (95%)
  between operations  1.93 us (5%)
    pallas_call x1, Pallas kernels, on_device(): pl.pallas_call(functools.partial(kernel, n_seq, n_head, n_dp), out_shape=...  35.6 us
    pallas_call x1, Pallas kernels, on_device(): pl.pallas_call(functools.partial(writer, len(shapes)), out_shape=shapes,...  2.05 us

profile of v2, /device:TPU:1, one launch (start us, length us, event | category | flops | bytes accessed | tf_op | source)
XLA Modules:
  0.0 39.6 jit_solution(232942918139881921)
XLA Ops:
  1.9 35.6 %lightning.1 = (bf16[1,512,1024]{2,1,0:T(8,128)(2,1)S(1)}, bf16[1,512,1024]{2,1,0:T(8,128)(2,1)S(1)}, bf16[1,512,1024]{2,1,0:T(8,128)(2,1)S(1)}, bf16[1,512,1024]{2,1,0:T(8,128)(2,1)S(1)}, f32[8,128]{1,0:T(8,128)S(1)}) custom-call(s32[8]{0:T(128)} %decay_hbm.1, f32[1]{0:T(128)S(6)} %copy.15.adv_ref, s32[1]{0:T(128)S(6)} %copy.16.len_ref, f32[8,128]{1,0:T(8,128)} %bitcast.2, ...), custom_call_target="tpu_custom_call" | custom-call | tf_op jit(solution)/shard_map/lightning/pallas_call | solution.py:664
  37.6 2.1 %writer.1 = (bf16[1,512,1024]{2,1,0:T(8,128)(2,1)}, bf16[1,512,1024]{2,1,0:T(8,128)(2,1)}, bf16[1,512,1024]{2,1,0:T(8,128)(2,1)}, bf16[1,512,1024]{2,1,0:T(8,128)(2,1)}, f32[8,128]{1,0:T(8,128)}) custom-call(bf16[1,512,1024]{2,1,0:T(8,128)(2,1)S(1)} %get-tuple-element.15.refs_0_, bf16[1,512,1024]{2,1,0:T(8,128)(2,1)S(1)} %get-tuple-element.16.refs_1_, ...), custom_call_target="tpu_custom_call" | custom-call | tf_op jit(solution)/shard_map/writer/pallas_call | solution.py:729

commit v3 on v2

--- a/solution.py
+++ b/solution.py
@@ -82,6 +82,7 @@
     gs_sem,
     gr_sem,
     turn,
+    ready,
 ):
     slab, features = q.shape
     heads = decay_ref.shape[0]
@@ -131,14 +132,26 @@
     kv_load(0, 1).start()
 
     barrier = pltpu.get_barrier_semaphore()
-    for off in range(1, n_seq):
-        pl.semaphore_signal(
-            barrier, inc=1, device_id={"seq": lax.rem(me + off, n_seq)}, device_id_type=MESH
-        )
-    for off in range(1, n_head):
-        pl.semaphore_signal(
-            barrier, inc=1, device_id={"head": lax.rem(mh + off, n_head)}, device_id_type=MESH
-        )
+    if square:
+        for s in range(stages):
+            pl.semaphore_signal(barrier, inc=1, device_id={"seq": partner(s)}, device_id_type=MESH)
+    else:
+        for off in range(1, n_seq):
+            pl.semaphore_signal(
+                barrier, inc=1, device_id={"seq": lax.rem(me + off, n_seq)}, device_id_type=MESH
+            )
+    near_heads = (mh > 0).astype(jnp.int32) + (mh < n_head - 1).astype(jnp.int32)
+
+    def greet(sem):
+        @pl.when(mh > 0)
+        def _():
+            pl.semaphore_signal(sem, inc=1, device_id={"head": mh - 1}, device_id_type=MESH)
+
+        @pl.when(mh < n_head - 1)
+        def _():
+            pl.semaphore_signal(sem, inc=1, device_id={"head": mh + 1}, device_id_type=MESH)
+
+    greet(barrier)
     for off in range(1, n_dp):
         pl.semaphore_signal(
             barrier, inc=1, device_id={"dp": lax.rem(md + off, n_dp)}, device_id_type=MESH
@@ -332,12 +345,17 @@
     local(0)
     for load in loads:
         load.start()
-    pl.semaphore_wait(barrier, n_seq - 1 + n_head - 1 + n_dp - 1)
+    pl.semaphore_wait(barrier, (stages if square else n_seq - 1) + n_dp - 1 + near_heads)
     first = md == 0
 
     @pl.when(first)
     def _():
         begin_pair(forward, 0)
+
+    steps = max(n_head - 2, 1)
+    greet(ready.at[0])
+    if square:
+        pl.semaphore_signal(ready.at[0], inc=1, device_id={"seq": partner(0)}, device_id_type=MESH)
 
     @pl.loop(1, pairs)
     def _(i):
@@ -422,6 +440,9 @@
             accept_pair(forward, i)
 
     middle(forward)
+    for s in range(steps - 1):
+        pl.semaphore_wait(ready.at[s], near_heads + (1 if square and s == 0 else 0))
+        greet(ready.at[s + 1])
 
     loads[1].wait()
     for load in small[1:]:
@@ -475,6 +496,7 @@
         )
         for off in range(1, n_head)
     ]
+    pl.semaphore_wait(ready.at[steps - 1], near_heads + (1 if square and steps == 1 else 0))
     for post in posts:
         post.start()
     for post in posts:
@@ -543,7 +565,11 @@
     )
     for share in shares:
         share.start()
-    accept_pair(backward, 0)
+    late = min(1, pairs - 1)
+
+    @pl.when(first)
+    def _():
+        accept_pair(backward, 0)
 
     @pl.loop(0, pairs)
     def _(i):
@@ -575,9 +601,19 @@
 
         for ahead in (1, 2):
 
-            @pl.when(2 * i + ahead < pairs)
+            @pl.when(jnp.logical_and(first, 2 * i + ahead < pairs))
             def _(ahead=ahead):
                 accept_pair(backward, 2 * i + ahead)
+
+        @pl.when(jnp.logical_and(jnp.logical_not(first), i == late))
+        def _():
+            @pl.loop(0, late)
+            def _(p):
+                accept_pair(backward, p)
+
+        @pl.when(jnp.logical_and(jnp.logical_not(first), i >= late))
+        def _():
+            accept_pair(backward, i)
 
     for share in shares:
         share.wait_recv()
@@ -707,6 +743,7 @@
             dma((n_seq,)),
             dma((n_seq,)),
             pltpu.SemaphoreType.REGULAR,
+            pltpu.SemaphoreType.REGULAR((max(n_head - 2, 1),)),
         ],
         compiler_params=pltpu.CompilerParams(
             collective_id=0, has_side_effects=True, vmem_limit_bytes=48 << 20

time: 39.8 us -> 38.9 us (0.977)
  Pallas kernels: 37.7 us -> 36.8 us
    pallas_call x1, Pallas kernels: 35.6 us -> 34.7 us  [on_device(): pl.pallas_call(functools.partial(kernel, n_seq, n_head, n_dp), out_shape=...]
where the time goes in v3:
time: 38.9 us; the launch traced here: 38.7 us
  Pallas kernels  36.8 us (95%)
  between operations  1.93 us (5%)
    pallas_call x1, Pallas kernels, on_device(): pl.pallas_call(functools.partial(kernel, n_seq, n_head, n_dp), out_shape=...  34.7 us
    pallas_call x1, Pallas kernels, on_device(): pl.pallas_call(functools.partial(writer, len(shapes)), out_shape=shapes,...  2.05 us

profile of v3, /device:TPU:1, one launch (start us, length us, event | category | flops | bytes accessed | tf_op | source)
XLA Modules:
  0.0 38.7 jit_solution(5884732128835196075)
XLA Ops:
  1.9 34.7 %lightning.1 = (bf16[1,512,1024]{2,1,0:T(8,128)(2,1)S(1)}, bf16[1,512,1024]{2,1,0:T(8,128)(2,1)S(1)}, bf16[1,512,1024]{2,1,0:T(8,128)(2,1)S(1)}, bf16[1,512,1024]{2,1,0:T(8,128)(2,1)S(1)}, f32[8,128]{1,0:T(8,128)S(1)}) custom-call(s32[8]{0:T(128)} %decay_hbm.1, f32[1]{0:T(128)S(6)} %copy.15.adv_ref, s32[1]{0:T(128)S(6)} %copy.16.len_ref, f32[8,128]{1,0:T(8,128)} %bitcast.2, ...), custom_call_target="tpu_custom_call" | custom-call | tf_op jit(solution)/shard_map/lightning/pallas_call | solution.py:700
  36.7 2.1 %writer.1 = (bf16[1,512,1024]{2,1,0:T(8,128)(2,1)}, bf16[1,512,1024]{2,1,0:T(8,128)(2,1)}, bf16[1,512,1024]{2,1,0:T(8,128)(2,1)}, bf16[1,512,1024]{2,1,0:T(8,128)(2,1)}, f32[8,128]{1,0:T(8,128)}) custom-call(bf16[1,512,1024]{2,1,0:T(8,128)(2,1)S(1)} %get-tuple-element.15.refs_0_, bf16[1,512,1024]{2,1,0:T(8,128)(2,1)S(1)} %get-tuple-element.16.refs_1_, ...), custom_call_target="tpu_custom_call" | custom-call | tf_op jit(solution)/shard_map/writer/pallas_call | solution.py:766

commit v4 on v3

--- a/solution.py
+++ b/solution.py
@@ -127,10 +127,6 @@
             )
         )
     ]
-    small[0].start()
-    kv_load(0, 0).start()
-    kv_load(0, 1).start()
-
     barrier = pltpu.get_barrier_semaphore()
     if square:
         for s in range(stages):
@@ -152,6 +148,9 @@
             pl.semaphore_signal(sem, inc=1, device_id={"head": mh + 1}, device_id_type=MESH)
 
     greet(barrier)
+    small[0].start()
+    kv_load(0, 0).start()
+    kv_load(0, 1).start()
     for off in range(1, n_dp):
         pl.semaphore_signal(
             barrier, inc=1, device_id={"dp": lax.rem(md + off, n_dp)}, device_id_type=MESH
@@ -314,9 +313,9 @@
             def _(h, s=s):
                 accept(d, h, s)
 
-    def settle(d):
+    def settle(d, which):
         place = d[5]
-        for s in range(stages):
+        for s in which:
             for odd in range(2):
                 bit = stages - 1 - s if square and odd else s
                 if not (square and odd):
@@ -569,7 +568,9 @@
 
     @pl.when(first)
     def _():
-        accept_pair(backward, 0)
+        @pl.loop(0, min(2, pairs))
+        def _(i):
+            accept_pair(backward, i)
 
     @pl.loop(0, pairs)
     def _(i):
@@ -599,7 +600,7 @@
                 pk[past, cols(h)] = dot(dsc[odd][rest, past], q[rest, cols(h)], 0, 0)
                 pv[past, cols(h)] = dot(probs[odd][i, rest, past], go[rest, cols(h)], 0, 0)
 
-        for ahead in (1, 2):
+        for ahead in (2, 3):
 
             @pl.when(jnp.logical_and(first, 2 * i + ahead < pairs))
             def _(ahead=ahead):
@@ -640,6 +641,10 @@
         close(2 * i)
         close(2 * i + 1)
 
+    for post in posts + shares:
+        post.wait_send()
+    settle(forward, range(stages))
+    settle(backward, range(stages - 1))
     finish_even(backward, pairs - 1)
     close(heads - 2)
     finish_odd(backward, pairs - 1)
@@ -649,10 +654,7 @@
         gg_ref[...] = gpair[0] + gpair[1]
     else:
         gg_ref[...] = gpair[0]
-    for post in posts + shares:
-        post.wait_send()
-    settle(forward)
-    settle(backward)
+    settle(backward, range(stages - 1, stages))
 
 
 def writer(n, *refs):

time: 38.9 us -> 38.9 us (level)
  no operation moved by 1% of the time
where the time goes in v4:
time: 38.9 us; the launch traced here: 38.7 us
  Pallas kernels  36.8 us (95%)
  between operations  1.93 us (5%)
    pallas_call x1, Pallas kernels, on_device(): pl.pallas_call(functools.partial(kernel, n_seq, n_head, n_dp), out_shape=...  34.7 us
    pallas_call x1, Pallas kernels, on_device(): pl.pallas_call(functools.partial(writer, len(shapes)), out_shape=shapes,...  2.05 us

profile of v4, /device:TPU:1, one launch (start us, length us, event | category | flops | bytes accessed | tf_op | source)
XLA Modules:
  0.0 38.7 jit_solution(1813145698497158832)
XLA Ops:
  1.9 34.7 %lightning.1 = (bf16[1,512,1024]{2,1,0:T(8,128)(2,1)S(1)}, bf16[1,512,1024]{2,1,0:T(8,128)(2,1)S(1)}, bf16[1,512,1024]{2,1,0:T(8,128)(2,1)S(1)}, bf16[1,512,1024]{2,1,0:T(8,128)(2,1)S(1)}, f32[8,128]{1,0:T(8,128)S(1)}) custom-call(s32[8]{0:T(128)} %decay_hbm.1, f32[1]{0:T(128)S(6)} %copy.15.adv_ref, s32[1]{0:T(128)S(6)} %copy.16.len_ref, f32[8,128]{1,0:T(8,128)} %bitcast.2, ...), custom_call_target="tpu_custom_call" | custom-call | tf_op jit(solution)/shard_map/lightning/pallas_call | solution.py:702
  36.6 2.1 %writer.1 = (bf16[1,512,1024]{2,1,0:T(8,128)(2,1)}, bf16[1,512,1024]{2,1,0:T(8,128)(2,1)}, bf16[1,512,1024]{2,1,0:T(8,128)(2,1)}, bf16[1,512,1024]{2,1,0:T(8,128)(2,1)}, f32[8,128]{1,0:T(8,128)}) custom-call(bf16[1,512,1024]{2,1,0:T(8,128)(2,1)S(1)} %get-tuple-element.15.refs_0_, bf16[1,512,1024]{2,1,0:T(8,128)(2,1)S(1)} %get-tuple-element.16.refs_1_, ...), custom_call_target="tpu_custom_call" | custom-call | tf_op jit(solution)/shard_map/writer/pallas_call | solution.py:768

commit v5 on v3

--- a/solution.py
+++ b/solution.py
@@ -12,7 +12,7 @@
 f32 = jnp.float32
 bf16 = jnp.bfloat16
 MESH = pl.DeviceIdType.MESH
-TURN = 3
+TURN = 6
 
 
 def dot(a, b, ca, cb):
@@ -379,59 +379,57 @@
 
     t_at = lax.broadcasted_iota(jnp.int32, (blk, blk), 0)
     s_at = lax.broadcasted_iota(jnp.int32, (blk, blk), 1)
-    shift = min(TURN, pairs - 1)
+    shift = min(TURN, heads - 1)
+
+    def attend(h, odd, i):
+        r = rate(h, dim)
+        place = lax.broadcasted_iota(jnp.int32, (1, dim), 1).astype(f32)
+        front = up[h, pl.ds(0, blk), :]
+        near = jnp.concatenate(
+            [front * jnp.exp2(r * (place + float(b * dim))) for b in range(blk // dim)], axis=1
+        )
+        wtab[odd][i, 0] = jnp.where(t_at >= s_at, near, 0.0)
+        for d in range(1, nblk):
+            away = jnp.exp2(-r * float(blk * d))
+            wtab[odd][i, d] = near * jnp.concatenate([away] * (blk // dim), axis=1)
+        for a in range(nblk):
+            rows = pl.ds(a * blk, blk)
+            for b in range(a + 1):
+                past = pl.ds(b * blk, blk)
+                score = dot(q[rows, cols(h)], k[past, cols(h)], 1, 1)
+                probs[odd][i, rows, past] = (score * wtab[odd][i, a - b]).astype(bf16)
+        for a in range(nblk):
+            rows = pl.ds(a * blk, blk)
+            past = pl.ds(0, (a + 1) * blk)
+            out[rows, cols(h)] = dot(probs[odd][i, rows, past], v[past, cols(h)], 1, 0)
 
     @pl.loop(0, pairs)
     def _(i):
         for odd in range(2):
             h = 2 * i + odd
-            r = rate(h, dim)
-            place = lax.broadcasted_iota(jnp.int32, (1, dim), 1).astype(f32)
-            front = up[h, pl.ds(0, blk), :]
-            near = jnp.concatenate(
-                [front * jnp.exp2(r * (place + float(b * dim))) for b in range(blk // dim)],
-                axis=1,
-            )
-            wtab[odd][i, 0] = jnp.where(t_at >= s_at, near, 0.0)
-            for d in range(1, nblk):
-                away = jnp.exp2(-r * float(blk * d))
-                wtab[odd][i, d] = near * jnp.concatenate([away] * (blk // dim), axis=1)
-        for a in range(nblk):
-            rows = pl.ds(a * blk, blk)
-            for odd in range(2):
-                h = 2 * i + odd
-                for b in range(a + 1):
-                    past = pl.ds(b * blk, blk)
-                    score = dot(q[rows, cols(h)], k[past, cols(h)], 1, 1)
-                    probs[odd][i, rows, past] = (score * wtab[odd][i, a - b]).astype(bf16)
-        for a in range(nblk):
-            rows = pl.ds(a * blk, blk)
-            past = pl.ds(0, (a + 1) * blk)
-            for odd in range(2):
-                h = 2 * i + odd
-                out[rows, cols(h)] = dot(probs[odd][i, rows, past], v[past, cols(h)], 1, 0)
-
-        for ahead in (1, 0):
-
-            @pl.when(jnp.logical_and(first, (2 * i - ahead >= 0) & (2 * i - ahead < pairs)))
-            def _(ahead=ahead):
-                accept_pair(forward, 2 * i - ahead)
-
-        if n_dp > 1:
-
-            @pl.when(jnp.logical_and(first, i == shift))
-            def _():
-                pl.semaphore_signal(turn, inc=1, device_id={"dp": 1 - md}, device_id_type=MESH)
-
-            @pl.when(jnp.logical_and(jnp.logical_not(first), i == shift))
-            def _():
-                pl.semaphore_wait(turn, 1)
-
-                @pl.loop(0, pairs)
-                def _(p):
-                    begin_pair(forward, p)
-
-                begin_rest(forward)
+            attend(h, odd, i)
+
+            @pl.when(jnp.logical_and(first, (h >= 1) & (h <= pairs)))
+            def _(h=h):
+                accept_pair(forward, h - 1)
+
+            if n_dp > 1:
+
+                @pl.when(jnp.logical_and(first, h == shift))
+                def _():
+                    pl.semaphore_signal(turn, inc=1, device_id={"dp": 1 - md}, device_id_type=MESH)
+
+    if n_dp > 1:
+
+        @pl.when(jnp.logical_not(first))
+        def _():
+            pl.semaphore_wait(turn, 1)
+
+            @pl.loop(0, pairs)
+            def _(i):
+                begin_pair(forward, i)
+
+            begin_rest(forward)
 
     @pl.when(jnp.logical_not(first))
     def _():

time: 38.9 us -> 38.9 us (level)
  no operation moved by 1% of the time
where the time goes in v5:
time: 38.9 us; the launch traced here: 38.7 us
  Pallas kernels  36.8 us (95%)
  between operations  1.93 us (5%)
    pallas_call x1, Pallas kernels, on_device(): pl.pallas_call(functools.partial(kernel, n_seq, n_head, n_dp), out_shape=...  34.7 us
    pallas_call x1, Pallas kernels, on_device(): pl.pallas_call(functools.partial(writer, len(shapes)), out_shape=shapes,...  2.05 us

profile of v5, /device:TPU:1, one launch (start us, length us, event | category | flops | bytes accessed | tf_op | source)
XLA Modules:
  0.0 38.7 jit_solution(17031709883027096152)
XLA Ops:
  1.9 34.7 %lightning.1 = (bf16[1,512,1024]{2,1,0:T(8,128)(2,1)S(1)}, bf16[1,512,1024]{2,1,0:T(8,128)(2,1)S(1)}, bf16[1,512,1024]{2,1,0:T(8,128)(2,1)S(1)}, bf16[1,512,1024]{2,1,0:T(8,128)(2,1)S(1)}, f32[8,128]{1,0:T(8,128)S(1)}) custom-call(s32[8]{0:T(128)} %decay_hbm.1, f32[1]{0:T(128)S(6)} %copy.15.adv_ref, s32[1]{0:T(128)S(6)} %copy.16.len_ref, f32[8,128]{1,0:T(8,128)} %bitcast.2, ...), custom_call_target="tpu_custom_call" | custom-call | tf_op jit(solution)/shard_map/lightning/pallas_call | solution.py:698
  36.6 2.1 %writer.1 = (bf16[1,512,1024]{2,1,0:T(8,128)(2,1)}, bf16[1,512,1024]{2,1,0:T(8,128)(2,1)}, bf16[1,512,1024]{2,1,0:T(8,128)(2,1)}, bf16[1,512,1024]{2,1,0:T(8,128)(2,1)}, f32[8,128]{1,0:T(8,128)}) custom-call(bf16[1,512,1024]{2,1,0:T(8,128)(2,1)S(1)} %get-tuple-element.15.refs_0_, bf16[1,512,1024]{2,1,0:T(8,128)(2,1)S(1)} %get-tuple-element.16.refs_1_, ...), custom_call_target="tpu_custom_call" | custom-call | tf_op jit(solution)/shard_map/writer/pallas_call | solution.py:764
